TPU v7x, 128 devices: a whole 4x4x4 slice. The times are simulated.
128 devices in a mesh: fsdp: 8 (over z_lo, x), dp: 4 (over y), cand: 4 (over z_hi, core).
Axes of the slice: x: 4, y: 4, z: 4 (z_hi: 2, z_lo: 2; z = z_hi * 2 + z_lo), core: 2. Of those that a mesh axis runs over, the one named last changes fastest.
Arguments:
- tokens: bfloat16 [640, 8192], P(('dp', 'cand'), 'fsdp'), may hold values from -6 to 6
- cotangent: bfloat16 [640, 8192], P(('dp', 'cand'), 'fsdp'), may hold values from -6 to 6
- bleu_gains: int32 [4, 8], P('dp', 'cand'), may hold values from 0 to 9600, as said below
- gate_weight: bfloat16 [8192, 29568], P('fsdp', ('dp', 'cand')), may hold values from -0.0625 to 0.0625
- up_weight: bfloat16 [8192, 29568], P('fsdp', ('dp', 'cand')), may hold values from -0.0625 to 0.0625
- down_weight: bfloat16 [29568, 8192], P(('dp', 'cand'), 'fsdp'), may hold values from -0.03125 to 0.03125
Outputs:
- layer_out: bfloat16 [640, 8192], P(('dp', 'cand'), 'fsdp')
- grad_tokens: bfloat16 [640, 8192], P(('dp', 'cand'), 'fsdp')
- grad_gate_weight: bfloat16 [8192, 29568], P('fsdp', ('dp', 'cand'))
- grad_up_weight: bfloat16 [8192, 29568], P('fsdp', ('dp', 'cand'))
- grad_down_weight: bfloat16 [29568, 8192], P(('dp', 'cand'), 'fsdp')
Inputs may be any that keep to these rules, and one draw needn't show every extreme that they name: `bleu_gains`: BLEU gain of a candidate in parts per ten thousand.
All inputs are finite; a program needn't handle non-finite values.
Results may differ from a plain program's by a relative error of at most 0.0058.
Values may be sent and summed in bfloat16 or wider, within the bound.
No kernel may reach another device: no remote copies, remote signals or barrier semaphores. Data moves between devices by JAX's collectives and lax.ppermute only.
A program may use at most 128 MiB of HBM per device.

v0:
```python
import jax
import jax.numpy as jnp
from jax import lax
from jax.sharding import PartitionSpec as P

CANDS = 8


def swiglu_backward(back_sum, gate_sum, up_sum):
    sigmoid_gate = jax.nn.sigmoid(gate_sum)
    grad_gate = (back_sum * up_sum * sigmoid_gate * (1.0 + gate_sum * (1.0 - sigmoid_gate))).astype(
        jnp.bfloat16
    )
    grad_up = (back_sum * (gate_sum * sigmoid_gate)).astype(jnp.bfloat16)
    return (grad_gate, grad_up)


def swiglu_forward(gate_sum, up_sum):
    return (gate_sum * jax.nn.sigmoid(gate_sum) * up_sum).astype(jnp.bfloat16)


def on_device(tokens, cotangent, bleu_gains, gate_weight, up_weight, down_weight):
    own_rows = tokens.shape[0]
    seq_len = own_rows // bleu_gains.size
    contract_cols = (((1,), (1,)), ((), ()))
    contract_rows = (((0,), (0,)), ((), ()))
    tok_all = lax.all_gather(tokens, ("dp", "cand"), axis=0, tiled=True)
    shifted = (bleu_gains + 1).astype(jnp.float32)
    totals = lax.psum(jnp.sum(shifted, axis=1), "cand")
    row_scale = jnp.repeat((CANDS * shifted / totals[:, None]).reshape(-1), seq_len)
    grad_own = (row_scale[:, None] * cotangent).astype(jnp.bfloat16)
    grad_all = lax.all_gather(grad_own, ("dp", "cand"), axis=0, tiled=True)
    gate_part = jnp.dot(tok_all, gate_weight, preferred_element_type=jnp.float32)
    up_part = jnp.dot(tok_all, up_weight, preferred_element_type=jnp.float32)
    gate_sum, up_sum = lax.psum((gate_part, up_part), "fsdp")
    hidden = swiglu_forward(gate_sum, up_sum)
    layer_out = lax.psum_scatter(
        jnp.dot(hidden, down_weight, preferred_element_type=jnp.float32),
        ("dp", "cand"),
        scatter_dimension=0,
        tiled=True,
    ).astype(jnp.bfloat16)
    back_part = lax.dot_general(
        grad_all, down_weight, contract_cols, preferred_element_type=jnp.float32
    )
    back_sum = lax.psum(back_part, "fsdp")
    grad_gate, grad_up = swiglu_backward(back_sum, gate_sum, up_sum)
    grad_down_weight = lax.dot_general(
        hidden, grad_all, contract_rows, preferred_element_type=jnp.float32
    ).astype(jnp.bfloat16)
    grad_gate_weight = lax.dot_general(
        tok_all, grad_gate, contract_rows, preferred_element_type=jnp.float32
    ).astype(jnp.bfloat16)
    grad_up_weight = lax.dot_general(
        tok_all, grad_up, contract_rows, preferred_element_type=jnp.float32
    ).astype(jnp.bfloat16)
    from_gate = lax.dot_general(
        grad_gate, gate_weight, contract_cols, preferred_element_type=jnp.float32
    )
    from_up = lax.dot_general(grad_up, up_weight, contract_cols, preferred_element_type=jnp.float32)
    grad_tokens = lax.psum_scatter(
        from_gate + from_up, ("dp", "cand"), scatter_dimension=0, tiled=True
    ).astype(jnp.bfloat16)
    return (layer_out, grad_tokens, grad_gate_weight, grad_up_weight, grad_down_weight)


def solution(mesh):
    return jax.shard_map(
        on_device,
        mesh=mesh,
        in_specs=(
            P(("dp", "cand"), "fsdp"),
            P(("dp", "cand"), "fsdp"),
            P("dp", "cand"),
            P("fsdp", ("dp", "cand")),
            P("fsdp", ("dp", "cand")),
            P(("dp", "cand"), "fsdp"),
        ),
        out_specs=(
            P(("dp", "cand"), "fsdp"),
            P(("dp", "cand"), "fsdp"),
            P("fsdp", ("dp", "cand")),
            P("fsdp", ("dp", "cand")),
            P(("dp", "cand"), "fsdp"),
        ),
        check_vma=False,
    )
```

profile of v0, /device:TPU:0, one launch (start us, length us, event | category | flops | bytes accessed | tf_op | source)
XLA Modules:
  0.0 578.3 jit_solution(13196504414203694526)
XLA Ops:
  7.2 0.0 all-gather.3.cloned.1.call-start
  7.2 0.7 all-gather.3.cloned.1.call-update
  7.9 0.0 all-gather.5.cloned.1.call-start
  7.9 1.3 convert_reduce_fusion
  9.2 11.5 %psum.30 = f32[]{:T(128)} all-reduce(f32[]{:T(128)} %convert_reduce_fusion), channel_id=1, replica_groups=mesh['fsdp'=8,'dp'=4,'cand'=4] {'cand'}, use_global_device_ids=true, to_apply=%region_4.0 | all-reduce | flops 1 | bytes 8 | tf_op jit(solution)/shard_map/psum | solution.py:29
  20.7 1.3 divide_bitcast_fusion
  22.0 0.1 broadcast_in_dim.4
  22.1 0.1 mul.38
  22.1 1.6 multiply_convert_fusion.3
  23.7 0.0 all-gather.5.cloned.1.call-update
  23.8 0.0 all-reduce.3.cloned.1.call-start
  23.8 35.1 %all-gather.3.cloned.1.call-done = bf16[640,1024]{1,0:T(8,128)(2,1)} async-done(((bf16[40,1024]{1,0:T(8,128)(2,1)}), bf16[640,1024]{1,0:T(8,128)(2,1)}) %all-gather.3.cloned.1.call-update) | async-done | bytes 1310736 | tf_op jit(solution)/shard_map/all_gather | solution.py:27
  58.9 7.9 %fusion.2 = f32[640,1848]{0,1:T(8,128)} fusion(bf16[640,1024]{1,0:T(8,128)(2,1)} %all-gather.3.cloned.1.call-done, bf16[1024,1848]{0,1:T(8,128)(2,1)} %param.10), kind=kOutput, calls=%fused_computation.13 | convolution fusion | flops 2422210560 | bytes 9826304 | tf_op jit(solution)/shard_map/dot_general | solution.py:34
  66.8 4.9 fusion.1
  71.7 34.9 %all-gather.5.cloned.1.call-done = bf16[640,1024]{1,0:T(8,128)(2,1)} async-done(((bf16[40,1024]{1,0:T(8,128)(2,1)}), bf16[640,1024]{1,0:T(8,128)(2,1)}) %all-gather.5.cloned.1.call-update) | async-done | bytes 1310736 | tf_op jit(solution)/shard_map/all_gather | solution.py:32
  106.5 7.9 %fusion.4 = f32[640,1848]{0,1:T(8,128)} fusion(bf16[640,1024]{1,0:T(8,128)(2,1)} %all-gather.5.cloned.1.call-done, bf16[1848,1024]{1,0:T(8,128)(2,1)} %param.11), kind=kOutput, calls=%fused_computation.15 | convolution fusion | flops 2422210560 | bytes 9826304 | tf_op jit(solution)/shard_map/dot_general | solution.py:43
  114.4 0.0 all-reduce.3.cloned.1.call-update
  114.4 0.0 reduce-scatter.3.cloned.1.call-start
  114.5 293.4 %all-reduce.3.cloned.1.call-done = (f32[640,1848]{0,1:T(8,128)}, f32[640,1848]{0,1:T(8,128)}, f32[640,1848]{0,1:T(8,128)}) async-done(((f32[640,1848]{0,1:T(8,128)}, f32[640,1848]{0,1:T(8,128)}, f32[640,1848]{0,1:T(8,128)}), (f32[640,1848]{0,1:T(8,128)}, f32[640,1848]{0,1:T(8,128)}, f32[640,1848]{0,1:T(8,128)})) %all-reduce.3.cloned.1.call-update) | async-done | bytes 14192656 | tf_op jit(solution)/shard_map/psum | solution.py:35
  407.8 7.6 %multiply_convert_fusion = (bf16[640,1848]{0,1:T(8,128)(2,1)S(1)}, bf16[640,1848]{0,1:T(8,128)(2,1)}, bf16[640,1848]{0,1:T(8,128)(2,1)S(1)}) fusion(f32[640,1848]{0,1:T(8,128)} %get-tuple-element.7, f32[640,1848]{0,1:T(8,128)} %get-tuple-element.6, f32[640,1848]{0,1:T(8,128)} %get-tuple-element.5), kind=kLoop, calls=%fused_computation | loop fusion | flops 17740800 | bytes 21288960 | tf_op jit(solution)/shard_map/convert_element_type | solution.py:14
  415.4 1.4 copy-done.2
  416.8 4.5 fusion.3
  421.3 0.2 reduce-scatter.5.cloned.1.call-start
  421.6 5.9 %fusion.5 = f32[640,1024]{1,0:T(8,128)S(1)} fusion(bf16[640,1848]{0,1:T(8,128)(2,1)} %get-tuple-element.9, bf16[1024,1848]{0,1:T(8,128)(2,1)} %param.9), kind=kOutput, calls=%fused_computation.16 | convolution fusion | flops 2422210560 | bytes 8771584 | tf_op jit(solution)/shard_map/dot_general | solution.py:57
  427.5 4.5 convolution_add_fusion
  432.1 7.3 %convolution_convert_fusion = bf16[1848,1024]{1,0:T(8,128)(2,1)} fusion(bf16[640,1848]{0,1:T(8,128)(2,1)} %copy-done.2, bf16[640,1024]{1,0:T(8,128)(2,1)} %all-gather.5.cloned.1.call-done), kind=kOutput, calls=%fused_computation.7 | convolution fusion | flops 2424102912 | bytes 7460864 | tf_op jit(solution)/shard_map/dot_general | solution.py:48
  439.3 4.6 convert_bitcast_fusion
  443.9 4.6 convert_bitcast_fusion.1
  448.5 45.2 %reduce-scatter.3.cloned.1.call-done = f32[40,1024]{1,0:T(8,128)} async-done(((f32[640,1024]{1,0:T(8,128)}), f32[40,1024]{1,0:T(8,128)}) %reduce-scatter.3.cloned.1.call-update) | async-done | bytes 163856 | tf_op jit(solution)/shard_map/reduce_scatter | solution.py:37
  493.7 1.6 convert_element_type.40
  495.3 75.0 %reduce-scatter.5.cloned.1.call-done = f32[40,1024]{1,0:T(8,128)} async-done(((f32[640,1024]{1,0:T(8,128)}), f32[40,1024]{1,0:T(8,128)}) %reduce-scatter.5.cloned.1.call-update) | async-done | bytes 163856 | tf_op jit(solution)/shard_map/reduce_scatter | solution.py:61
  570.2 1.6 convert_element_type.46
  (15 shorter events, 0.1 us)
Async XLA Ops:
  7.2 51.8 %all-gather.3.cloned.1.call-start = ((), (), s32[]{:S(2)}) async-start(), calls=%async_computation.2 | async-start | bytes 1392640 | tf_op jit(solution)/shard_map/all_gather | solution.py:27
  7.9 98.6 %all-gather.5.cloned.1.call-start = ((), (), s32[]{:S(2)}) async-start(), calls=%async_computation.4 | async-start | bytes 1392640 | tf_op jit(solution)/shard_map/all_gather | solution.py:32
  23.8 384.1 %all-reduce.3.cloned.1.call-start = ((), (), s32[]{:S(2)}) async-start(), calls=%async_computation.6 | async-start | bytes 28385280 | tf_op jit(solution)/shard_map/psum | solution.py:35
  58.9 7.9 %copy-start.4 = (bf16[1024,1848]{0,1:T(8,128)(2,1)S(1)}, bf16[1024,1848]{0,1:T(8,128)(2,1)}, u32[]{:S(2)}) copy-start(bf16[1024,1848]{0,1:T(8,128)(2,1)} %param.9) | copy-start | bytes 11354116
  58.9 7.9 %copy-start.5 = (bf16[640,1024]{1,0:T(8,128)(2,1)S(1)}, bf16[640,1024]{1,0:T(8,128)(2,1)}, u32[]{:S(2)}) copy-start(bf16[640,1024]{1,0:T(8,128)(2,1)} %all-gather.3.cloned.1.call-done) | copy-start | bytes 3932164
  114.4 379.3 %reduce-scatter.3.cloned.1.call-start = ((), (), s32[]{:S(2)}) async-start(), calls=%async_computation.3 | async-start | bytes 2785280 | tf_op jit(solution)/shard_map/reduce_scatter | solution.py:37
  407.8 9.0 %copy-start.3 = (bf16[1848,1024]{1,0:T(8,128)(2,1)S(1)}, bf16[1848,1024]{1,0:T(8,128)(2,1)}, u32[]{:S(2)}) copy-start(bf16[1848,1024]{1,0:T(8,128)(2,1)} %param.11) | copy-start | bytes 11354116
  415.4 1.4 copy-start.2
  421.3 148.9 %reduce-scatter.5.cloned.1.call-start = ((), (), s32[]{:S(2)}) async-start(), calls=%async_computation.5 | async-start | bytes 2785280 | tf_op jit(solution)/shard_map/reduce_scatter | solution.py:61
  421.6 5.9 %copy-start = (bf16[1024,1848]{0,1:T(8,128)(2,1)S(1)}, bf16[1024,1848]{0,1:T(8,128)(2,1)}, u32[]{:S(2)}) copy-start(bf16[1024,1848]{0,1:T(8,128)(2,1)} %param.10) | copy-start | bytes 11354116
  432.0 7.3 %copy-start.6 = (bf16[640,1024]{1,0:T(8,128)(2,1)S(1)}, bf16[640,1024]{1,0:T(8,128)(2,1)}, u32[]{:S(2)}) copy-start(bf16[640,1024]{1,0:T(8,128)(2,1)} %all-gather.3.cloned.1.call-done) | copy-start | bytes 3932164
  439.3 4.6 copy-start.1
Sparse Core Ops, SparseCore 0:
  10.4 48.4 all-gather.2
  61.9 44.5 all-gather.4
  114.5 293.2 all-reduce.2
  421.4 72.2 reduce-scatter.2
  498.1 72.1 reduce-scatter.4
where the time goes:
time: 579 us; the launch traced here: 578 us
  waiting for transfers between devices  484 us (84%)
  matrix products  51.9 us (9%)
  other arithmetic  14.9 us (3%)
  between operations  13.8 us (2%)
  blocking collectives  11.5 us (2%)
    psum x1, waiting for transfers between devices, on_device(): gate_sum, up_sum = lax.psum((gate_part, up_part), 'fsdp')  293 us
    reduce_scatter x1, waiting for transfers between devices, on_device(): lax.psum_scatter(from_gate + from_up, ('dp', 'cand'), scatter_dimension=0...  75 us
    reduce_scatter x1, waiting for transfers between devices, on_device(): lax.psum_scatter(jnp.dot(hidden, down_weight, preferred_element_type=jnp....  45.2 us
    all_gather x1, waiting for transfers between devices, on_device(): tok_all = lax.all_gather(tokens, ('dp', 'cand'), axis=0, tiled=True)  35.1 us
    all_gather x1, waiting for transfers between devices, on_device(): grad_all = lax.all_gather(grad_own, ('dp', 'cand'), axis=0, tiled=True)  34.9 us
  transfers between devices with their start and end apart: 5, of which 5 were waited for; matrix products, arithmetic and copies ran while one was open for 8% of the time, Pallas kernels for 0%

commit v1 on v0

--- a/solution.py
+++ b/solution.py
@@ -24,7 +24,10 @@
     seq_len = own_rows // bleu_gains.size
     contract_cols = (((1,), (1,)), ((), ()))
     contract_rows = (((0,), (0,)), ((), ()))
-    tok_all = lax.all_gather(tokens, ("dp", "cand"), axis=0, tiled=True)
+    size = lax.axis_size(("dp", "cand"))
+    blocks = jnp.stack([tokens for _ in range(size)])
+    blocks = lax.all_to_all(blocks, ("dp", "cand"), split_axis=0, concat_axis=0)
+    tok_all = jnp.concatenate(blocks, axis=0)
     shifted = (bleu_gains + 1).astype(jnp.float32)
     totals = lax.psum(jnp.sum(shifted, axis=1), "cand")
     row_scale = jnp.repeat((CANDS * shifted / totals[:, None]).reshape(-1), seq_len)

time: 579 us -> 558 us (0.964)
  waiting for transfers between devices: 484 us -> 456 us
  starting transfers between devices: 0.38 us -> 8.32 us
    all_gather x1 -> x0, waiting for transfers between devices: 35.1 us -> none  [on_device(): tok_all = lax.all_gather(tokens, ('dp', 'cand'), axis=0, tiled=True)]
    all_to_all x0 -> x1, starting transfers between devices: none -> 7.97 us  [on_device(): blocks = lax.all_to_all(blocks, ('dp', 'cand'), split_axis=0, concat_axis=0)]
    all_to_all x0 -> x1, waiting for transfers between devices: none -> 7.07 us  [on_device(): blocks = lax.all_to_all(blocks, ('dp', 'cand'), split_axis=0, concat_axis=0)]
  transfers between devices with their start and end apart: 5 -> 5, of which waited for: 5 -> 5; matrix products, arithmetic and copies ran while one was open for 8% -> 7% of each run, Pallas kernels for 0% -> 0%
where the time goes in v1:
time: 558 us
  waiting for transfers between devices  456 us (82%)
  matrix products  50.6 us (9%)
  between operations  13.9 us (2%)
  other arithmetic  13.4 us (2%)
  blocking collectives  12.1 us (2%)
  starting transfers between devices  8.32 us (1%)
    psum x1, waiting for transfers between devices, on_device(): gate_sum, up_sum = lax.psum((gate_part, up_part), 'fsdp')  293 us
    reduce_scatter x1, waiting for transfers between devices, on_device(): lax.psum_scatter(from_gate + from_up, ('dp', 'cand'), scatter_dimension=0...  75 us
    reduce_scatter x1, waiting for transfers between devices, on_device(): lax.psum_scatter(jnp.dot(hidden, down_weight, preferred_element_type=jnp....  46.3 us
    all_gather x1, waiting for transfers between devices, on_device(): grad_all = lax.all_gather(grad_own, ('dp', 'cand'), axis=0, tiled=True)  34 us
    psum x1, blocking collectives, on_device(): totals = lax.psum(jnp.sum(shifted, axis=1), 'cand')  12.1 us
  transfers between devices with their start and end apart: 5, of which 5 were waited for; matrix products, arithmetic and copies ran while one was open for 7% of the time, Pallas kernels for 0%

profile of v1, /device:TPU:0, one launch (start us, length us, event | category | flops | bytes accessed | tf_op | source)
XLA Modules:
  0.0 557.8 jit_solution(9164979560017737502)
XLA Ops:
  7.2 1.3 convert_reduce_fusion
  8.5 2.1 stack.2
  10.6 8.0 %all-to-all-start = ((bf16[16,40,1024]{2,1,0:T(8,128)(2,1)}), bf16[16,40,1024]{2,1,0:T(8,128)(2,1)S(1)}, u32[]{:S(2)}, u32[]{:S(2)}) async-start(bf16[16,40,1024]{2,1,0:T(8,128)(2,1)} %stack.2), calls=%async_computation | async-start | bytes 2621440 | tf_op jit(solution)/shard_map/all_to_all | solution.py:29
  18.6 0.0 all-gather.2.cloned.1.call-start
  18.6 12.1 %psum.30 = f32[]{:T(128)} all-reduce(f32[]{:T(128)} %convert_reduce_fusion), channel_id=1, replica_groups=mesh['fsdp'=8,'dp'=4,'cand'=4] {'cand'}, use_global_device_ids=true, to_apply=%region_4.0 | all-reduce | flops 1 | bytes 8 | tf_op jit(solution)/shard_map/psum | solution.py:32
  30.7 0.7 divide_bitcast_fusion
  31.4 0.1 broadcast_in_dim.4
  31.4 0.1 mul.38
  31.5 0.7 multiply_convert_fusion.3
  32.2 0.0 all-gather.2.cloned.1.call-update
  32.3 0.0 all-reduce.3.cloned.1.call-start
  32.3 7.1 %all-to-all-done = bf16[16,40,1024]{2,1,0:T(8,128)(2,1)S(1)} async-done(((bf16[16,40,1024]{2,1,0:T(8,128)(2,1)}), bf16[16,40,1024]{2,1,0:T(8,128)(2,1)S(1)}, u32[]{:S(2)}, u32[]{:S(2)}) %all-to-all-start) | async-done | bytes 1310752 | tf_op jit(solution)/shard_map/all_to_all | solution.py:29
  39.4 7.9 %fusion.2 = f32[640,1848]{0,1:T(8,128)} fusion(bf16[640,1024]{1,0:T(8,128)(2,1)S(1)} %bitcast.25, bf16[1024,1848]{0,1:T(8,128)(2,1)} %param.10), kind=kOutput, calls=%fused_computation.13 | convolution fusion | flops 2422210560 | bytes 9826304 | tf_op jit(solution)/shard_map/dot_general | solution.py:37
  47.2 4.8 fusion.1
  52.0 34.0 %all-gather.2.cloned.1.call-done = bf16[640,1024]{1,0:T(8,128)(2,1)} async-done(((bf16[40,1024]{1,0:T(8,128)(2,1)}), bf16[640,1024]{1,0:T(8,128)(2,1)}) %all-gather.2.cloned.1.call-update) | async-done | bytes 1310736 | tf_op jit(solution)/shard_map/all_gather | solution.py:35
  86.1 7.8 %fusion.4 = f32[640,1848]{0,1:T(8,128)} fusion(bf16[640,1024]{1,0:T(8,128)(2,1)} %all-gather.2.cloned.1.call-done, bf16[1848,1024]{1,0:T(8,128)(2,1)} %param.11), kind=kOutput, calls=%fused_computation.15 | convolution fusion | flops 2422210560 | bytes 9826304 | tf_op jit(solution)/shard_map/dot_general | solution.py:46
  93.9 0.0 all-reduce.3.cloned.1.call-update
  93.9 0.0 reduce-scatter.3.cloned.1.call-start
  94.0 293.4 %all-reduce.3.cloned.1.call-done = (f32[640,1848]{0,1:T(8,128)}, f32[640,1848]{0,1:T(8,128)}, f32[640,1848]{0,1:T(8,128)}) async-done(((f32[640,1848]{0,1:T(8,128)}, f32[640,1848]{0,1:T(8,128)}, f32[640,1848]{0,1:T(8,128)}), (f32[640,1848]{0,1:T(8,128)}, f32[640,1848]{0,1:T(8,128)}, f32[640,1848]{0,1:T(8,128)})) %all-reduce.3.cloned.1.call-update) | async-done | bytes 14192656 | tf_op jit(solution)/shard_map/psum | solution.py:38
  387.3 7.6 %multiply_convert_fusion = (bf16[640,1848]{0,1:T(8,128)(2,1)S(1)}, bf16[640,1848]{0,1:T(8,128)(2,1)}, bf16[640,1848]{0,1:T(8,128)(2,1)S(1)}) fusion(f32[640,1848]{0,1:T(8,128)} %get-tuple-element.7, f32[640,1848]{0,1:T(8,128)} %get-tuple-element.6, f32[640,1848]{0,1:T(8,128)} %get-tuple-element.5), kind=kLoop, calls=%fused_computation | loop fusion | flops 17740800 | bytes 21288960 | tf_op jit(solution)/shard_map/convert_element_type | solution.py:14
  394.9 1.5 copy-done.1
  396.3 4.4 fusion.3
  400.8 0.2 reduce-scatter.5.cloned.1.call-start
  401.0 5.9 %fusion.5 = f32[640,1024]{1,0:T(8,128)S(1)} fusion(bf16[640,1848]{0,1:T(8,128)(2,1)} %get-tuple-element.9, bf16[1024,1848]{0,1:T(8,128)(2,1)} %param.9), kind=kOutput, calls=%fused_computation.16 | convolution fusion | flops 2422210560 | bytes 8771584 | tf_op jit(solution)/shard_map/dot_general | solution.py:60
  406.9 4.6 convolution_add_fusion
  411.6 6.1 %convert_bitcast_fusion = bf16[1024,1848]{0,1:T(8,128)(2,1)} fusion(bf16[640,1848]{0,1:T(8,128)(2,1)S(1)} %get-tuple-element.8, bf16[640,1024]{1,0:T(8,128)(2,1)} %bitcast.27), kind=kOutput, calls=%fused_computation.5 | convolution fusion | flops 2424102912 | bytes 7460864 | tf_op jit(solution)/shard_map/dot_general | solution.py:57
  417.7 4.6 convert_bitcast_fusion.1
  422.3 4.6 convolution_convert_fusion
  426.8 46.3 %reduce-scatter.3.cloned.1.call-done = f32[40,1024]{1,0:T(8,128)} async-done(((f32[640,1024]{1,0:T(8,128)}), f32[40,1024]{1,0:T(8,128)}) %reduce-scatter.3.cloned.1.call-update) | async-done | bytes 163856 | tf_op jit(solution)/shard_map/reduce_scatter | solution.py:40
  473.2 1.6 convert_element_type.40
  474.7 75.0 %reduce-scatter.5.cloned.1.call-done = f32[40,1024]{1,0:T(8,128)} async-done(((f32[640,1024]{1,0:T(8,128)}), f32[40,1024]{1,0:T(8,128)}) %reduce-scatter.5.cloned.1.call-update) | async-done | bytes 163856 | tf_op jit(solution)/shard_map/reduce_scatter | solution.py:64
  549.7 1.6 convert_element_type.46
  (23 shorter events, 0.1 us)
Async XLA Ops:
  7.2 23.5 %copy-start.10 = (s32[1,2]{1,0:T(1,128)S(1)}, s32[1,2]{1,0:T(1,128)}, u32[]{:S(2)}) copy-start(s32[1,2]{1,0:T(1,128)} %param.8) | copy-start | bytes 28
  7.2 24.3 %copy-start.6 = (bf16[40,1024]{1,0:T(8,128)(2,1)S(1)}, bf16[40,1024]{1,0:T(8,128)(2,1)}, u32[]{:S(2)}) copy-start(bf16[40,1024]{1,0:T(8,128)(2,1)} %param.7) | copy-start | bytes 245764
  10.6 28.8 %all-to-all-start = ((bf16[16,40,1024]{2,1,0:T(8,128)(2,1)}), bf16[16,40,1024]{2,1,0:T(8,128)(2,1)S(1)}, u32[]{:S(2)}, u32[]{:S(2)}) async-start(bf16[16,40,1024]{2,1,0:T(8,128)(2,1)} %stack.2), calls=%async_computation | async-start | bytes 2621440 | tf_op jit(solution)/shard_map/all_to_all | solution.py:29
  18.6 67.5 %all-gather.2.cloned.1.call-start = ((), (), s32[]{:S(2)}) async-start(), calls=%async_computation.4 | async-start | bytes 1392640 | tf_op jit(solution)/shard_map/all_gather | solution.py:35
  32.3 355.1 %all-reduce.3.cloned.1.call-start = ((), (), s32[]{:S(2)}) async-start(), calls=%async_computation.6 | async-start | bytes 28385280 | tf_op jit(solution)/shard_map/psum | solution.py:38
  39.4 7.9 %copy-start.4 = (bf16[16,40,1024]{2,1,0:T(8,128)(2,1)}, bf16[16,40,1024]{2,1,0:T(8,128)(2,1)S(1)}, u32[]{:S(2)}) copy-start(bf16[16,40,1024]{2,1,0:T(8,128)(2,1)S(1)} %all-to-all-done) | copy-start | bytes 3932164
  39.4 7.9 %copy-start.8 = (bf16[1024,1848]{0,1:T(8,128)(2,1)S(1)}, bf16[1024,1848]{0,1:T(8,128)(2,1)}, u32[]{:S(2)}) copy-start(bf16[1024,1848]{0,1:T(8,128)(2,1)} %param.9) | copy-start | bytes 11354116
  93.9 379.3 %reduce-scatter.3.cloned.1.call-start = ((), (), s32[]{:S(2)}) async-start(), calls=%async_computation.3 | async-start | bytes 2785280 | tf_op jit(solution)/shard_map/reduce_scatter | solution.py:40
  387.3 9.0 %copy-start.7 = (bf16[1848,1024]{1,0:T(8,128)(2,1)S(1)}, bf16[1848,1024]{1,0:T(8,128)(2,1)}, u32[]{:S(2)}) copy-start(bf16[1848,1024]{1,0:T(8,128)(2,1)} %param.11) | copy-start | bytes 11354116
  394.9 1.5 copy-start.1
  400.8 149.0 %reduce-scatter.5.cloned.1.call-start = ((), (), s32[]{:S(2)}) async-start(), calls=%async_computation.5 | async-start | bytes 2785280 | tf_op jit(solution)/shard_map/reduce_scatter | solution.py:64
  401.0 5.9 %copy-start = (bf16[1024,1848]{0,1:T(8,128)(2,1)S(1)}, bf16[1024,1848]{0,1:T(8,128)(2,1)}, u32[]{:S(2)}) copy-start(bf16[1024,1848]{0,1:T(8,128)(2,1)} %param.10) | copy-start | bytes 11354116
  411.5 6.1 %copy-start.3 = (bf16[640,1848]{0,1:T(8,128)(2,1)S(1)}, bf16[640,1848]{0,1:T(8,128)(2,1)}, u32[]{:S(2)}) copy-start(bf16[640,1848]{0,1:T(8,128)(2,1)} %get-tuple-element.9) | copy-start | bytes 7096324
  411.6 6.1 %copy-start.5 = (bf16[16,40,1024]{2,1,0:T(8,128)(2,1)S(1)}, bf16[16,40,1024]{2,1,0:T(8,128)(2,1)}, u32[]{:S(2)}) copy-start(bf16[16,40,1024]{2,1,0:T(8,128)(2,1)} %copy-done.4) | copy-start | bytes 3932164
  417.7 4.6 copy-start.2
  417.7 4.6 copy-start.9
Sparse Core Ops, SparseCore 0:
  32.4 53.6 all-gather.1
  94.0 293.2 all-reduce.2
  400.9 72.2 reduce-scatter.2
  477.5 72.1 reduce-scatter.4
